TPU v7x, 256 devices: a whole 4x4x8 slice. The times are simulated.
256 devices in a mesh: seq: 32 (over z, x), dp: 8 (over y, core).
Axes of the slice: x: 4, y: 4, z: 8, core: 2. Of those that a mesh axis runs over, the one named last changes fastest.
Arguments:
- tokens: bfloat16 [8, 16384, 4096], P('dp', 'seq'), may hold values from -6 to 6
- w_in: bfloat16 [4096, 2336], P(('seq', 'dp')), may hold values from -0.09375 to 0.09375
- conv_w: float32 [4, 2304], replicated, may hold values from -3 to 3
- a_rate: float32 [32], replicated, may hold values from 3.0517579e-06 to 0.06
- d_skip: float32 [32], replicated, may hold values from 0.5 to 2
- level_w: int32 [8, 11], P('dp'), may hold values from 0 to 256
- lengths: int32 [8], P('dp'), may hold values from 64 to 16384, as said below
Outputs:
- mixed_out: bfloat16 [8, 16384, 2048], P('dp', 'seq')
Inputs may be any that keep to these rules, and one draw needn't show every extreme that they name: `lengths`: every length is a multiple of 64, and some request has all 16384 positions live.
All inputs are finite; a program needn't handle non-finite values.
Results may differ from a plain program's by a relative error of at most 0.015.
Values may be sent and summed in bfloat16 or wider, within the bound.
No kernel may reach another device: no remote copies, remote signals or barrier semaphores. Data moves between devices by JAX's collectives and lax.ppermute only.
A program may use at most 128 MiB of HBM per device.

v0:
```python
import jax
import jax.numpy as jnp
import numpy as np
from jax import lax
from jax.sharding import PartitionSpec as P

STATE = 128
Q = 64


def passed_along(array, axis, by):
    count = lax.axis_size(axis)
    pairs = [(i, i + by) for i in range(count) if 0 <= i + by < count]
    return lax.ppermute(array, axis, pairs)


def swapped(value, axis, stride):
    mask = 2**stride
    pairs = [(source, source ^ mask) for source in range(lax.axis_size(axis))]
    return lax.ppermute(value, axis, pairs)


def body(tokens, w_in, conv_w, a_rate, d_skip, level_w, lengths):
    token_rows = tokens.reshape(-1, tokens.shape[-1])
    count = token_rows.shape[0]
    projected = jnp.dot(
        token_rows,
        lax.all_gather(w_in, ("seq", "dp"), axis=0, tiled=True),
        preferred_element_type=jnp.float32,
    )
    kernel = conv_w.shape[0]
    channels = conv_w.shape[1]
    heads = a_rate.shape[0]
    inner = channels - 2 * STATE
    raw = projected[:, :channels].astype(jnp.bfloat16)
    rim = passed_along(raw[count - (kernel - 1) :], "seq", 1)
    padded = jnp.concatenate([rim, raw], 0)
    convolved = jnp.zeros((count, channels), jnp.float32)
    for offset in range(kernel):
        convolved = convolved + padded[offset : offset + count].astype(jnp.float32) * conv_w[offset]
    values = jax.nn.silu(convolved[:, :inner]).astype(jnp.bfloat16)
    in_b = convolved[:, inner : inner + STATE].astype(jnp.bfloat16)
    out_c = convolved[:, inner + STATE :].astype(jnp.bfloat16)
    step_size = jax.nn.softplus(projected[:, channels:])
    log_decay = -step_size * a_rate[None, :]
    head_dim = inner // heads
    driven = (
        values.astype(jnp.float32).reshape(count, heads, head_dim) * step_size[:, :, None]
    ).astype(jnp.bfloat16)
    stretches = count // Q
    cumul = jnp.cumsum(log_decay.reshape(stretches, Q, heads), axis=1)
    totals = cumul[:, -1]
    before = jnp.cumsum(totals, axis=0) - totals
    level_wt = level_w.reshape(-1).astype(jnp.float32) / 256.0
    keys_b = in_b.reshape(stretches, Q, STATE)
    query_c = out_c.reshape(stretches, Q, STATE)
    drive_c = driven.reshape(stretches, Q, heads, head_dim)
    scores = jnp.einsum("ctn,csn->cts", query_c, keys_b, preferred_element_type=jnp.float32)
    causal = jnp.asarray(np.tril(np.ones((Q, Q), bool)))[None, :, :, None]
    differ = cumul[:, :, None, :] - cumul[:, None, :, :]
    inner_wt = (
        jnp.where(causal, jnp.exp(jnp.where(causal, differ, 0.0)), 0.0)
        * scores[..., None]
        * level_wt[0]
    )
    inner_wt = inner_wt.astype(jnp.bfloat16)
    y_inner = jnp.einsum("ctsh,cshp->cthp", inner_wt, drive_c, preferred_element_type=jnp.float32)
    to_end = jnp.exp(totals[:, None, :] - cumul)
    weighted_b = (keys_b.astype(jnp.float32)[:, :, None, :] * to_end[..., None]).astype(
        jnp.bfloat16
    )
    states = jnp.einsum("cshn,cshp->chnp", weighted_b, drive_c, preferred_element_type=jnp.float32)
    local_bits = stretches.bit_length() - 1
    carried = jnp.zeros_like(states)
    block_states = states
    block_decay = totals
    stretch_ids = np.arange(stretches)
    for level in range(local_bits):
        span = 2**level
        repeated = jnp.repeat(block_states, span, axis=0)
        previous = jnp.concatenate(
            [jnp.zeros_like(repeated[:span]), repeated[: stretches - span]], 0
        )
        bit_set = jnp.asarray((stretch_ids >> level & 1).astype(np.float32))
        aligned = stretch_ids >> level << level
        factor = bit_set[:, None] * level_wt[level + 1] * jnp.exp(before - before[aligned])
        carried = carried + factor[:, :, None, None] * previous
        block_states = (
            block_states[0::2] * jnp.exp(block_decay[1::2])[:, :, None, None] + block_states[1::2]
        )
        block_decay = block_decay[0::2] + block_decay[1::2]
    block_state = block_states[0]
    block_total = block_decay[0]
    position = lax.axis_index("seq")
    cross_state = jnp.zeros_like(block_state)
    passed = jnp.zeros_like(block_total)
    seq_bits = lax.axis_size("seq").bit_length() - 1
    for level in range(seq_bits):
        other_state, other_total = (
            swapped(block_state.astype(jnp.bfloat16), "seq", level).astype(block_state.dtype),
            swapped(block_total.astype(jnp.bfloat16), "seq", level).astype(block_total.dtype),
        )
        upper = (jnp.right_shift(position, level) & 1).astype(jnp.float32)
        cross_state = (
            cross_state
            + upper
            * level_wt[local_bits + level + 1]
            * jnp.exp(passed)[:, None, None]
            * other_state
        )
        passed = passed + upper * other_total
        block_state = jnp.where(
            upper > 0.5,
            other_state * jnp.exp(block_total)[:, None, None] + block_state,
            block_state * jnp.exp(other_total)[:, None, None] + other_state,
        )
        block_total = block_total + other_total
    carried = carried + jnp.exp(before)[:, :, None, None] * cross_state[None]
    carried_low = carried.astype(jnp.bfloat16)
    y_cross = jnp.exp(cumul)[..., None] * jnp.einsum(
        "ctn,chnp->cthp", query_c, carried_low, preferred_element_type=jnp.float32
    )
    output = (
        y_inner
        + y_cross
        + d_skip[None, None, :, None]
        * values.astype(jnp.float32).reshape(stretches, Q, heads, head_dim)
    )
    output = output * lax.rsqrt(jnp.mean(output * output, axis=-1, keepdims=True) + 1e-05)
    places = (position * count + jnp.arange(count, dtype=jnp.int32)).reshape(stretches, Q)
    output = jnp.where((places < lengths[0])[:, :, None, None], output, 0.0)
    return output.reshape(1, count, inner).astype(jnp.bfloat16)


def solution(mesh):
    in_specs = (P("dp", "seq", None), P(("seq", "dp"), None), P(), P(), P(), P("dp", None), P("dp"))
    out_specs = P("dp", "seq", None)
    return jax.shard_map(body, mesh=mesh, in_specs=in_specs, out_specs=out_specs, check_vma=False)
```

profile of v0, /device:TPU:5, one launch (start us, length us, event | category | flops | bytes accessed | tf_op | source)
XLA Modules:
  0.0 375.2 jit_solution(5178389369494430748)
XLA Ops:
  6.5 0.7 all-gather.2.cloned.1.call-update
  8.6 1.0 slice_reduce_fusion.3
  9.6 133.8 %all-gather.2.cloned.1.call-done = bf16[4096,2336]{1,0:T(8,128)(2,1)} async-done(((bf16[16,2336]{1,0:T(8,128)(2,1)}), bf16[4096,2336]{1,0:T(8,128)(2,1)}) %all-gather.2.cloned.1.call-update) | async-done | bytes 19136528 | tf_op jit(solution)/shard_map/all_gather | solution.py:28
  143.4 18.0 %fusion.50 = (bf16[512,2336]{0,1:T(8,128)(2,1)S(1)}, f32[512,2336]{0,1:T(8,128)}) fusion(bf16[4096,2336]{1,0:T(8,128)(2,1)} %all-gather.2.cloned.1.call-done, bf16[1,512,4096]{2,1,0:T(8,128)(2,1)} %param.17), kind=kOutput, calls=%fused_computation.119 | convolution fusion | flops 9799090176 | bytes 30507008 | tf_op jit(solution)/shard_map/dot_general | solution.py:26
  161.4 1.0 compare_select_fusion
  162.6 6.3 %fusion.51 = f32[8,64,32]{2,0,1:T(8,128)S(1)} fusion(f32[8,64,32]{2,0,1:T(8,128)S(1)} %copy.43), kind=kOutput, calls=%fused_computation.120 | output fusion | flops 1032192 | bytes 131072 | tf_op jit(solution)/shard_map/jit(cumsum)/reduce_window_sum | solution.py:51
  169.0 0.9 fusion.46
  170.4 3.1 collective-permute-start
  174.1 1.8 slice.189
  177.2 5.9 %fusion.44 = (bf16[512,2304]{0,1:T(8,128)(2,1)S(1)}, f32[512,2304]{0,1:T(8,128)}) fusion(f32[2304]{0:T(1024)S(1)} %get-tuple-element.7, bf16[512,2304]{0,1:T(8,128)(2,1)S(1)} %slice.189, f32[2304]{0:T(1024)S(1)} %get-tuple-element.8, bf16[3,2304]{0,1:T(8,128)(2,1)S(1)} %copy.40, f32[2304]{0:T(1024)S(1)} %get-tuple-element.6, f32[2304]{0:T(1024)S(1)} %get-tuple-element.5), kind=kLoop, calls=%fused_computation.113 | loop fusion | flops 24772608 | bytes 9487872 | tf_op jit(solution)/shard_map/convert.2
  183.9 5.3 %fusion.15 = f32[512,2048]{0,1:T(8,128)} fusion(f32[512,2304]{0,1:T(8,128)} %get-tuple-element.20), kind=kLoop, calls=%fused_computation.33 | loop fusion | flops 6291456 | bytes 8388608 | tf_op jit(solution)/shard_map/reshape | solution.py:48
  189.2 7.2 %reshape.221 = f32[8,64,32,64]{1,0,3,2:T(8,128)} reshape(f32[512,2048]{0,1:T(8,128)} %fusion.15) | data formatting | bytes 8388608 | tf_op jit(solution)/shard_map/reshape | solution.py:48
  196.4 6.3 %fusion.2 = f32[8,32,128,64]{2,3,1,0:T(8,128)S(1)} fusion(f32[8,64,32]{1,2,0:T(8,128)S(1)} %copy.49, f32[8,64,128]{2,1,0:T(8,128)S(1)} %convert_element_type.135, f32[8,64,32,64]{1,0,3,2:T(8,128)} %reshape.221, f32[8,64,32]{1,2,0:T(8,128)S(1)} %copy-done.11), kind=kOutput, calls=%fused_computation.13 | convolution fusion | flops 274726912 | bytes 12976128 | tf_op jit(solution)/shard_map/cshn,cshp->chnp/dot_general | solution.py:72
  203.2 2.8 copy-done
  206.2 1.4 fusion.30
  208.6 1.1 collective-permute-start.2
  210.3 10.8 %collective-permute-done.2 = bf16[32]{0:T(256)(128)(2,1)S(1)} collective-permute-done((bf16[32]{0:T(256)(128)(2,1)S(1)}, bf16[32]{0:T(256)(128)(2,1)S(1)}, u32[]{:S(2)}, u32[]{:S(2)}) %collective-permute-start.2) | collective-permute-done | bytes 96 | tf_op jit(solution)/shard_map/ppermute | solution.py:20
  222.4 2.8 collective-permute-done.4
  225.2 1.3 exponential_multiply_fusion.5
  226.4 0.8 copy-done.8
  227.2 2.3 fusion.42
  232.0 9.9 %collective-permute-done.3 = bf16[32,128,64]{1,2,0:T(8,128)(2,1)S(1)} collective-permute-done((bf16[32,128,64]{1,2,0:T(8,128)(2,1)}, bf16[32,128,64]{1,2,0:T(8,128)(2,1)S(1)}, u32[]{:S(2)}, u32[]{:S(2)}) %collective-permute-start.3) | collective-permute-done | bytes 524320 | tf_op jit(solution)/shard_map/ppermute | solution.py:20
  244.0 1.1 collective-permute-start.6
  245.7 6.5 %collective-permute-done.6 = bf16[32]{0:T(256)(128)(2,1)S(1)} collective-permute-done((bf16[32]{0:T(256)(128)(2,1)S(1)}, bf16[32]{0:T(256)(128)(2,1)S(1)}, u32[]{:S(2)}, u32[]{:S(2)}) %collective-permute-start.6) | collective-permute-done | bytes 96 | tf_op jit(solution)/shard_map/ppermute | solution.py:20
  252.8 1.3 collective-permute-start.8
  254.7 1.5 collective-permute-done.8
  256.2 1.2 exponential_multiply_fusion.4
  257.3 2.1 fusion.37
  259.4 1.2 collective-permute-start.7
  261.3 1.3 broadcast_multiply_fusion.2
  262.6 1.9 broadcast_multiply_fusion
  264.6 20.6 %collective-permute-done.7 = bf16[32,128,64]{1,2,0:T(8,128)(2,1)S(1)} collective-permute-done((bf16[32,128,64]{1,2,0:T(8,128)(2,1)}, bf16[32,128,64]{1,2,0:T(8,128)(2,1)S(1)}, u32[]{:S(2)}, u32[]{:S(2)}) %collective-permute-start.7) | collective-permute-done | bytes 524320 | tf_op jit(solution)/shard_map/ppermute | solution.py:20
  285.2 2.6 fusion.28
  287.8 3.0 collective-permute-start.9
  290.8 0.8 copy.44
  293.2 0.8 copy.48
  294.1 0.9 copy-done.13
  295.1 0.9 fusion.52
  296.1 21.0 %collective-permute-done.9 = bf16[32,128,64]{1,2,0:T(8,128)(2,1)} collective-permute-done((bf16[32,128,64]{1,2,0:T(8,128)(2,1)}, bf16[32,128,64]{1,2,0:T(8,128)(2,1)}, u32[]{:S(2)}, u32[]{:S(2)}) %collective-permute-start.9) | collective-permute-done | bytes 524320 | tf_op jit(solution)/shard_map/ppermute | solution.py:20
  317.1 3.2 fusion.19
  320.3 4.0 %broadcast_in_dim.37 = f32[3,2,32,128,64]{3,4,2,1,0:T(8,128)} broadcast(f32[3,32,128,64]{2,3,1,0:T(8,128)S(1)} %slice-done.3), dimensions={0,2,3,4} | broadcast | bytes 9437184 | tf_op jit(solution)/shard_map/broadcast_in_dim | solution.py:80
  324.3 2.7 slice.172
  327.5 7.6 %add_convert_fusion = bf16[8,32,128,64]{2,3,1,0:T(8,128)(2,1)} fusion(f32[4,32,128,64]{2,3,1,0:T(8,128)} %slice.172, f32[6,32,128,64]{2,3,1,0:T(8,128)} %bitcast.73, f32[7,32,128,64]{2,3,1,0:T(8,128)S(1)} %slice-done, f32[32,128,64]{1,2,0:T(8,128)S(1)} %copy-done.4, f32[8,32]{1,0:T(8,128)S(1)} %get-tuple-element.9, f32[8,32]{1,0:T(8,128)S(1)} %get-tuple-element.30, ...), kind=kLoop, calls=%fused_computation.7 | loop fusion | flops 16777216 | bytes 23072768 | tf_op jit(solution)/shard_map/convert_element_type | solution.py:119
  335.1 3.5 fusion.53
  338.7 8.8 %multiply_reduce_fusion = (f32[8,64,32]{1,2,0:T(8,128)S(1)}, f32[8,64,32,64]{1,3,2,0:T(8,128)}) fusion(f32[8,64,32,64]{1,0,3,2:T(8,128)S(1)} %bitcast.70, f32[32]{0:T(128)S(1)} %copy-done.22, f32[8,64,32,64]{1,3,2,0:T(8,128)S(1)} %bitcast.72, f32[8,64,32]{1,2,0:T(8,128)S(1)} %copy-done.16, f32[]{:T(128)} %bitcast.4, f32[8,64,64]{2,1,0:T(8,128)S(1)} %copy-done.14, ...), kind=kOutput, calls=%fused_computation.6 | convolution fusion | flops 148881408 | bytes 12980356 | tf_op jit(solution)/shard_map/ctsh,cshp->cthp/dot_general | solution.py:67
  347.5 7.0 %select_convert_fusion = bf16[8,64,32,64]{1,3,2,0:T(8,128)(2,1)} fusion(f32[8,64,32,64]{1,3,2,0:T(8,128)} %get-tuple-element.60, f32[8,64,32]{1,2,0:T(8,128)S(1)} %add_rsqrt_fusion, pred[8,64]{1,0:T(8,128)(4,1)S(1)} %copy-done.17), kind=kLoop, calls=%fused_computation.5 | loop fusion | flops 3145728 | bytes 6357504 | tf_op jit(solution)/shard_map/convert_element_type | solution.py:132
  354.5 7.1 %copy.51 = bf16[8,64,32,64]{3,2,1,0:T(8,128)(2,1)} copy(bf16[8,64,32,64]{1,3,2,0:T(8,128)(2,1)} %select_convert_fusion) | data formatting | bytes 4194304 | tf_op jit(solution)/shard_map/convert_element_type | solution.py:132
  361.6 6.7 %convert_element_type.162 = bf16[1,512,2048]{2,1,0:T(8,128)(2,1)} reshape(bf16[8,64,32,64]{3,2,1,0:T(8,128)(2,1)} %copy.51) | data formatting | bytes 4194304 | tf_op jit(solution)/shard_map/convert_element_type | solution.py:132
  (104 shorter events, 14.2 us)
Async XLA Ops:
  6.5 136.9 %all-gather.2.cloned.1.call-start = ((), (), s32[]{:S(2)}) async-start(), calls=%async_computation | async-start | bytes 20000768 | tf_op jit(solution)/shard_map/all_gather | solution.py:28
  9.6 151.7 %copy-start.20 = (f32[32]{0:T(128)S(1)}, f32[32]{0:T(128)}, u32[]{:S(2)}) copy-start(f32[32]{0:T(128)} %param.20) | copy-start | bytes 388
  161.4 12.2 %copy-start.6 = (bf16[512,2336]{0,1:T(8,128)(2,1)}, bf16[512,2336]{0,1:T(8,128)(2,1)S(1)}, u32[]{:S(2)}) copy-start(bf16[512,2336]{0,1:T(8,128)(2,1)S(1)} %get-tuple-element.57) | copy-start | bytes 7176196
  169.9 36.3 %copy-start.19 = (f32[32]{0:T(128)}, f32[32]{0:T(128)S(1)}, u32[]{:S(2)}) copy-start(f32[32]{0:T(128)S(1)} %exponential_bitcast_fusion) | copy-start | bytes 388
  170.4 6.3 %copy-start.10 = (f32[8,64,32]{2,0,1:T(8,128)S(1)}, f32[8,64,32]{2,0,1:T(8,128)}, u32[]{:S(2)}) copy-start(f32[8,64,32]{2,0,1:T(8,128)} %get-tuple-element.28) | copy-start | bytes 196612
  170.4 6.4 %collective-permute-start = (bf16[3,2304]{1,0:T(4,128)(2,1)S(1)}, bf16[3,2304]{1,0:T(4,128)(2,1)S(1)}, u32[]{:S(2)}, u32[]{:S(2)}) collective-permute-start(bf16[3,2304]{1,0:T(4,128)(2,1)S(1)} %copy.39), channel_id=1, source_target_pairs={{0,8},{8,16},{16,24},{24,32},{32,40},{40,48},{48,56},{56,64},{64,7... | collective-permute-start | bytes 41480 | tf_op jit(solution)/shard_map/ppermute | solution.py:14
  174.1 47.1 %copy-start.18 = (f32[1,32]{1,0:T(1,128)}, f32[1,32]{1,0:T(1,128)S(1)}, u32[]{:S(2)}) copy-start(f32[1,32]{1,0:T(1,128)S(1)} %get-tuple-element.18) | copy-start | bytes 388
  189.2 7.2 %copy-start.11 = (f32[8,64,32]{1,2,0:T(8,128)S(1)}, f32[8,64,32]{1,2,0:T(8,128)}, u32[]{:S(2)}) copy-start(f32[8,64,32]{1,2,0:T(8,128)} %copy.41) | copy-start | bytes 196612
  202.7 3.2 copy-start
  205.9 2.3 copy-start.1
  208.2 18.2 %collective-permute-start.1 = (bf16[32,128,64]{1,2,0:T(8,128)(2,1)S(1)}, bf16[32,128,64]{1,2,0:T(8,128)(2,1)S(1)}, u32[]{:S(2)}, u32[]{:S(2)}) collective-permute-start(bf16[32,128,64]{1,2,0:T(8,128)(2,1)S(1)} %get-tuple-element.25), channel_id=1, source_target_pairs={{0,8},{8,0},{16,24},{24,16},{32,40},{40,32},{48,56},{56,48},{64,72... | collective-permute-start | bytes 1572872 | tf_op jit(solution)/shard_map/ppermute | solution.py:20
  208.6 12.6 %collective-permute-start.2 = (bf16[32]{0:T(256)(128)(2,1)S(1)}, bf16[32]{0:T(256)(128)(2,1)S(1)}, u32[]{:S(2)}, u32[]{:S(2)}) collective-permute-start(bf16[32]{0:T(256)(128)(2,1)S(1)} %bitcast_convert_fusion), channel_id=1, source_target_pairs={{0,8},{8,0},{16,24},{24,16},{32,40},{40,32},{48,56},{56,48},{64,72... | collective-permute-start | bytes 200 | tf_op jit(solution)/shard_map/ppermute | solution.py:20
  221.2 1.2 copy-start.21
  221.2 4.0 %collective-permute-start.4 = (bf16[32]{0:T(256)(128)(2,1)S(1)}, bf16[32]{0:T(256)(128)(2,1)}, u32[]{:S(2)}, u32[]{:S(2)}) collective-permute-start(bf16[32]{0:T(256)(128)(2,1)S(1)} %fusion.36), channel_id=1, source_target_pairs={{0,16},{8,24},{16,0},{24,8},{32,48},{40,56},{48,32},{56,40},{64,80... | collective-permute-start | bytes 200 | tf_op jit(solution)/shard_map/ppermute | solution.py:20
  226.4 0.8 copy-start.8
  229.5 63.7 %copy-start.9 = (f32[8,64,32]{2,0,1:T(8,128)S(1)}, f32[8,64,32]{2,0,1:T(8,128)}, u32[]{:S(2)}) copy-start(f32[8,64,32]{2,0,1:T(8,128)} %get-tuple-element.27) | copy-start | bytes 196612
  229.5 12.4 %collective-permute-start.3 = (bf16[32,128,64]{1,2,0:T(8,128)(2,1)}, bf16[32,128,64]{1,2,0:T(8,128)(2,1)S(1)}, u32[]{:S(2)}, u32[]{:S(2)}) collective-permute-start(bf16[32,128,64]{1,2,0:T(8,128)(2,1)} %get-tuple-element.15), channel_id=1, source_target_pairs={{0,16},{8,24},{16,0},{24,8},{32,48},{40,56},{48,32},{56,40},{64,80... | collective-permute-start | bytes 1572872 | tf_op jit(solution)/shard_map/ppermute | solution.py:20
  241.9 52.2 %copy-start.2 = (bf16[32,128,64]{1,2,0:T(8,128)(2,1)}, bf16[32,128,64]{1,2,0:T(8,128)(2,1)S(1)}, u32[]{:S(2)}) copy-start(bf16[32,128,64]{1,2,0:T(8,128)(2,1)S(1)} %collective-permute-done.3) | copy-start | bytes 1572868
  242.3 15.1 %collective-permute-start.5 = (bf16[32,128,64]{1,2,0:T(8,128)(2,1)S(1)}, bf16[32,128,64]{1,2,0:T(8,128)(2,1)S(1)}, u32[]{:S(2)}, u32[]{:S(2)}) collective-permute-start(bf16[32,128,64]{1,2,0:T(8,128)(2,1)S(1)} %fusion.38), channel_id=1, source_target_pairs={{0,32},{8,40},{16,48},{24,56},{32,0},{40,8},{48,16},{56,24},{64,96... | collective-permute-start | bytes 1572872 | tf_op jit(solution)/shard_map/ppermute | solution.py:20
  244.0 8.2 %collective-permute-start.6 = (bf16[32]{0:T(256)(128)(2,1)S(1)}, bf16[32]{0:T(256)(128)(2,1)S(1)}, u32[]{:S(2)}, u32[]{:S(2)}) collective-permute-start(bf16[32]{0:T(256)(128)(2,1)S(1)} %convert_element_type.151), channel_id=1, source_target_pairs={{0,32},{8,40},{16,48},{24,56},{32,0},{40,8},{48,16},{56,24},{64,96... | collective-permute-start | bytes 200 | tf_op jit(solution)/shard_map/ppermute | solution.py:20
  252.8 3.3 collective-permute-start.8
  257.3 36.8 %copy-start.3 = (bf16[32,128,64]{1,2,0:T(8,128)(2,1)}, bf16[32,128,64]{1,2,0:T(8,128)(2,1)S(1)}, u32[]{:S(2)}) copy-start(bf16[32,128,64]{1,2,0:T(8,128)(2,1)S(1)} %collective-permute-done.5) | copy-start | bytes 1572868
  259.4 25.7 %collective-permute-start.7 = (bf16[32,128,64]{1,2,0:T(8,128)(2,1)}, bf16[32,128,64]{1,2,0:T(8,128)(2,1)S(1)}, u32[]{:S(2)}, u32[]{:S(2)}) collective-permute-start(bf16[32,128,64]{1,2,0:T(8,128)(2,1)} %fusion.37), channel_id=1, source_target_pairs={{0,64},{8,72},{16,80},{24,88},{32,96},{40,104},{48,112},{56,120},{... | collective-permute-start | bytes 1572872 | tf_op jit(solution)/shard_map/ppermute | solution.py:20
  285.2 2.6 copy-start.7
  287.8 29.3 %collective-permute-start.9 = (bf16[32,128,64]{1,2,0:T(8,128)(2,1)}, bf16[32,128,64]{1,2,0:T(8,128)(2,1)}, u32[]{:S(2)}, u32[]{:S(2)}) collective-permute-start(bf16[32,128,64]{1,2,0:T(8,128)(2,1)} %fusion.28), channel_id=1, source_target_pairs={{0,128},{8,136},{16,144},{24,152},{32,160},{40,168},{48,176},{56,1... | collective-permute-start | bytes 1572872 | tf_op jit(solution)/shard_map/ppermute | solution.py:20
  294.1 0.9 copy-start.13
  294.1 26.1 %slice-start.3 = ((f32[4,32,128,64]{2,3,1,0:T(8,128)}), f32[3,32,128,64]{2,3,1,0:T(8,128)S(1)}, s32[]{:S(2)}) async-start(f32[4,32,128,64]{2,3,1,0:T(8,128)} %copy-done.1), calls=%async_computation.4 | async-start | bytes 6291456 | tf_op jit(solution)/shard_map/slice | solution.py:82
  320.3 4.0 %copy-start.5 = (f32[32,128,64]{1,2,0:T(8,128)S(1)}, f32[32,128,64]{1,2,0:T(8,128)}, u32[]{:S(2)}) copy-start(f32[32,128,64]{1,2,0:T(8,128)} %get-tuple-element.26) | copy-start | bytes 3145732
  320.3 6.7 %slice-start = ((f32[8,32,128,64]{2,3,1,0:T(8,128)}), f32[7,32,128,64]{2,3,1,0:T(8,128)S(1)}, s32[]{:S(2)}) async-start(f32[8,32,128,64]{2,3,1,0:T(8,128)} %copy-done), calls=%async_computation.1 | async-start | bytes 14680064 | tf_op jit(solution)/shard_map/slice | solution.py:82
  324.3 3.2 copy-start.4
  324.3 14.3 %slice-start.1 = ((s8[8388608]{0:T(1024)(128)(4,1)}), s8[4194304]{0:T(1024)(128)(4,1)S(1)}, s32[]{:S(2)}) async-start(s8[8388608]{0:T(1024)(128)(4,1)} %bitcast.69), calls=%async_computation.2 | async-start | bytes 8388608
  327.5 11.2 %slice-start.2 = ((s8[8388608]{0:T(1024)(128)(4,1)}), s8[4194304]{0:T(1024)(128)(4,1)S(1)}, s32[]{:S(2)}) async-start(s8[8388608]{0:T(1024)(128)(4,1)} %bitcast.69), calls=%async_computation.3 | async-start | bytes 8388608
  335.1 3.5 copy-start.12
  335.1 3.6 copy-start.14
  335.1 3.6 copy-start.15
  335.1 3.6 copy-start.16
  335.1 3.6 copy-start.22
  335.1 3.6 copy-start.23
  338.7 8.8 %copy-start.17 = (pred[8,64]{1,0:T(8,128)(4,1)S(1)}, pred[8,64]{1,0:T(8,128)(4,1)}, u32[]{:S(2)}) copy-start(pred[8,64]{1,0:T(8,128)(4,1)} %add_compare_fusion) | copy-start | bytes 1540
Sparse Core Ops, SparseCore 0:
  10.9 132.4 all-gather.1
where the time goes:
time: 376 us; the launch traced here: 375 us
  waiting for transfers between devices  208 us (55%)
  other arithmetic  56.9 us (15%)
  local copies, waits for them, and re-layouts  43.1 us (11%)
  matrix products  37.4 us (10%)
  between operations  17.3 us (5%)
  starting transfers between devices  12.8 us (3%)
    all_gather x1, waiting for transfers between devices, body(): lax.all_gather(w_in, ('seq', 'dp'), axis=0, tiled=True)  134 us
    ppermute x9, waiting for transfers between devices, swapped(): return lax.ppermute(value, axis, pairs)  73.2 us
    dot_general x1, matrix products, body(): jnp.dot(token_rows, lax.all_gather(w_in, ('seq', 'dp'), axis=0, tiled=Tru...  18 us
    convert_element_type x2, local copies, waits for them, and re-layouts, body(): return output.reshape(1, count, inner).astype(jnp.bfloat16)  13.9 us
    ppermute x9, starting transfers between devices, swapped(): return lax.ppermute(value, axis, pairs)  9.71 us
    dot_general x1, matrix products, body(): jnp.einsum('ctsh,cshp->cthp', inner_wt, drive_c, preferred_element_type=j...  8.75 us
    convert_element_type x5, other arithmetic, body(): block_state.astype(jnp.bfloat16)  8.74 us
    convert_element_type x1, other arithmetic, body(): carried_low = carried.astype(jnp.bfloat16)  7.62 us
  transfers between devices with their start and end apart: 11, of which 8 were waited for; matrix products, arithmetic and copies ran while one was open for 5% of the time, Pallas kernels for 0%

commit v1 on v0

--- a/solution.py
+++ b/solution.py
@@ -6,6 +6,13 @@
 
 STATE = 128
 Q = 64
+
+
+def all_by_exchange(array, axis, along):
+    size = lax.axis_size(axis)
+    pieces = jnp.stack([array for _ in range(size)])
+    pieces = lax.all_to_all(pieces, axis, split_axis=0, concat_axis=0)
+    return jnp.concatenate(pieces, axis=along)
 
 
 def passed_along(array, axis, by):
@@ -24,9 +31,7 @@
     token_rows = tokens.reshape(-1, tokens.shape[-1])
     count = token_rows.shape[0]
     projected = jnp.dot(
-        token_rows,
-        lax.all_gather(w_in, ("seq", "dp"), axis=0, tiled=True),
-        preferred_element_type=jnp.float32,
+        token_rows, all_by_exchange(w_in, ("seq", "dp"), 0), preferred_element_type=jnp.float32
     )
     kernel = conv_w.shape[0]
     channels = conv_w.shape[1]

time: 376 us -> 680 us (1.81)
  waiting for transfers between devices: 208 us -> 493 us
  starting transfers between devices: 12.8 us -> 36.4 us
  between operations: 17.3 us -> 4.23 us
  local copies, waits for them, and re-layouts: 43.1 us -> 51.1 us
    all_to_all x0 -> x1, waiting for transfers between devices: none -> 429 us  [all_by_exchange(): pieces = lax.all_to_all(pieces, axis, split_axis=0, concat_axis=0)]
    all_gather x1 -> x0, waiting for transfers between devices: 134 us -> none  [body(): lax.all_gather(w_in, ('seq', 'dp'), axis=0, tiled=True)]
    all_to_all x0 -> x1, starting transfers between devices: none -> 15.8 us  [all_by_exchange(): pieces = lax.all_to_all(pieces, axis, split_axis=0, concat_axis=0)]
    ppermute x9, waiting for transfers between devices: 73.2 us -> 64.6 us  [swapped(): return lax.ppermute(value, axis, pairs)]
    ppermute x9, starting transfers between devices: 9.71 us -> 17.6 us  [swapped(): return lax.ppermute(value, axis, pairs)]
    another operation x1 -> x2, local copies, waits for them, and re-layouts: 0.01 us -> 7.64 us  [the longest x1 7.64 us: all_by_exchange(): pieces = jnp.stack([array for _ in range(size)])]
  transfers between devices with their start and end apart: 11 -> 11, of which waited for: 8 -> 8; matrix products, arithmetic and copies ran while one was open for 5% -> 3% of each run, Pallas kernels for 0% -> 0%
where the time goes in v1:
time: 680 us; the launch traced here: 677 us
  waiting for transfers between devices  493 us (72%)
  other arithmetic  54.7 us (8%)
  local copies, waits for them, and re-layouts  51.1 us (8%)
  matrix products  37.2 us (5%)
  starting transfers between devices  36.4 us (5%)
    all_to_all x1, waiting for transfers between devices, all_by_exchange(): pieces = lax.all_to_all(pieces, axis, split_axis=0, concat_axis=0)  429 us
    ppermute x9, waiting for transfers between devices, swapped(): return lax.ppermute(value, axis, pairs)  64.6 us
    dot_general x1, matrix products, body(): jnp.dot(token_rows, all_by_exchange(w_in, ('seq', 'dp'), 0), preferred_el...  17.8 us
    ppermute x9, starting transfers between devices, swapped(): return lax.ppermute(value, axis, pairs)  17.6 us
    all_to_all x1, starting transfers between devices, all_by_exchange(): pieces = lax.all_to_all(pieces, axis, split_axis=0, concat_axis=0)  15.8 us
    convert_element_type x2, local copies, waits for them, and re-layouts, body(): return output.reshape(1, count, inner).astype(jnp.bfloat16)  13.9 us
  transfers between devices with their start and end apart: 11, of which 8 were waited for; matrix products, arithmetic and copies ran while one was open for 3% of the time, Pallas kernels for 0%

profile of v1, /device:TPU:5, one launch (start us, length us, event | category | flops | bytes accessed | tf_op | source)
XLA Modules:
  0.0 677.0 jit_solution(8666359385752030047)
XLA Ops:
  0.0 7.6 %stack.2 = bf16[256,16,2336]{2,1,0:T(8,128)(2,1)} broadcast(bf16[16,2336]{1,0:T(8,128)(2,1)} %param.18), dimensions={1,2} | broadcast | bytes 19211264 | tf_op jit(solution)/shard_map/stack | solution.py:13
  7.6 15.8 %all-to-all-start = ((bf16[256,16,2336]{2,1,0:T(8,128)(2,1)}), bf16[256,16,2336]{2,1,0:T(8,128)(2,1)}, u32[]{:S(2)}, u32[]{:S(2)}) async-start(bf16[256,16,2336]{2,1,0:T(8,128)(2,1)} %stack.2), calls=%async_computation | async-start | bytes 39845888 | tf_op jit(solution)/shard_map/all_to_all | solution.py:14
  25.0 428.8 %all-to-all-done = bf16[256,16,2336]{2,1,0:T(8,128)(2,1)} async-done(((bf16[256,16,2336]{2,1,0:T(8,128)(2,1)}), bf16[256,16,2336]{2,1,0:T(8,128)(2,1)}, u32[]{:S(2)}, u32[]{:S(2)}) %all-to-all-start) | async-done | bytes 19136544 | tf_op jit(solution)/shard_map/all_to_all | solution.py:14
  453.7 17.8 %fusion.50 = (bf16[512,2336]{0,1:T(8,128)(2,1)S(1)}, f32[512,2336]{0,1:T(8,128)}) fusion(bf16[4096,2336]{1,0:T(8,128)(2,1)} %bitcast.2, bf16[1,512,4096]{2,1,0:T(8,128)(2,1)} %param.17), kind=kOutput, calls=%fused_computation.119 | convolution fusion | flops 9799090176 | bytes 30507008 | tf_op jit(solution)/shard_map/dot_general | solution.py:33
  471.6 1.0 compare_select_fusion
  472.8 6.3 fusion.51
  479.3 0.9 fusion.46
  481.2 2.9 collective-permute-start
  484.6 1.8 slice.189
  487.7 5.9 fusion.44
  494.4 5.3 fusion.15
  499.7 7.2 %reshape.227 = f32[8,64,32,64]{1,0,3,2:T(8,128)} reshape(f32[512,2048]{0,1:T(8,128)} %fusion.15) | data formatting | bytes 8388608 | tf_op jit(solution)/shard_map/reshape | solution.py:53
  506.9 6.3 fusion.2
  513.7 2.8 copy-done
  517.0 1.5 fusion.30
  518.7 2.4 collective-permute-start.1
  521.7 9.4 %collective-permute-done.2 = bf16[32]{0:T(256)(128)(2,1)S(1)} collective-permute-done((bf16[32]{0:T(256)(128)(2,1)S(1)}, bf16[32]{0:T(256)(128)(2,1)S(1)}, u32[]{:S(2)}, u32[]{:S(2)}) %collective-permute-start.2) | collective-permute-done | bytes 96 | tf_op jit(solution)/shard_map/ppermute | solution.py:27
  531.1 1.6 collective-permute-start.4
  532.7 2.4 collective-permute-done.4
  535.1 1.3 exponential_multiply_fusion.5
  536.3 0.8 copy-done.5
  537.1 2.3 fusion.42
  539.4 1.5 collective-permute-start.3
  543.0 7.4 %collective-permute-done.3 = bf16[32,128,64]{1,2,0:T(8,128)(2,1)S(1)} collective-permute-done((bf16[32,128,64]{1,2,0:T(8,128)(2,1)}, bf16[32,128,64]{1,2,0:T(8,128)(2,1)S(1)}, u32[]{:S(2)}, u32[]{:S(2)}) %collective-permute-start.3) | collective-permute-done | bytes 524320 | tf_op jit(solution)/shard_map/ppermute | solution.py:27
  550.7 1.1 collective-permute-start.5
  554.2 4.9 collective-permute-done.6
  559.7 6.2 collective-permute-start.8
  566.9 1.3 exponential_multiply_fusion.4
  568.2 2.1 fusion.37
  570.3 2.4 collective-permute-start.7
  573.2 1.3 broadcast_multiply_fusion.2
  574.5 1.9 broadcast_multiply_fusion
  576.4 19.1 %collective-permute-done.7 = bf16[32,128,64]{1,2,0:T(8,128)(2,1)S(1)} collective-permute-done((bf16[32,128,64]{1,2,0:T(8,128)(2,1)}, bf16[32,128,64]{1,2,0:T(8,128)(2,1)S(1)}, u32[]{:S(2)}, u32[]{:S(2)}) %collective-permute-start.7) | collective-permute-done | bytes 524320 | tf_op jit(solution)/shard_map/ppermute | solution.py:27
  595.6 2.6 fusion.28
  598.2 2.1 collective-permute-start.9
  603.7 0.9 copy-done.10
  604.7 0.9 fusion.52
  605.6 21.0 %collective-permute-done.9 = bf16[32,128,64]{1,2,0:T(8,128)(2,1)} collective-permute-done((bf16[32,128,64]{1,2,0:T(8,128)(2,1)}, bf16[32,128,64]{1,2,0:T(8,128)(2,1)}, u32[]{:S(2)}, u32[]{:S(2)}) %collective-permute-start.9) | collective-permute-done | bytes 524320 | tf_op jit(solution)/shard_map/ppermute | solution.py:27
  626.6 1.9 fusion.19
  628.5 2.6 slice.172
  631.1 4.2 broadcast_in_dim.37
  635.4 1.1 slice-done
  636.5 7.3 %add_convert_fusion = bf16[8,32,128,64]{2,3,1,0:T(8,128)(2,1)} fusion(f32[4,32,128,64]{2,3,1,0:T(8,128)} %slice.172, f32[6,32,128,64]{2,3,1,0:T(8,128)} %bitcast.74, f32[7,32,128,64]{2,3,1,0:T(8,128)S(1)} %slice-done, f32[32,128,64]{1,2,0:T(8,128)S(1)} %fusion.19, f32[8,32]{1,0:T(8,128)S(1)} %get-tuple-element.9, f32[8,32]{1,0:T(8,128)S(1)} %get-tuple-element.30, ...), kind=kLoop, calls=%fused_computation.7 | loop fusion | flops 16777216 | bytes 23072768 | tf_op jit(solution)/shard_map/convert_element_type | solution.py:124
  643.8 3.5 fusion.53
  647.4 8.7 %multiply_reduce_fusion = (f32[8,64,32]{1,2,0:T(8,128)S(1)}, f32[8,64,32,64]{1,3,2,0:T(8,128)}) fusion(f32[8,64,32,64]{1,0,3,2:T(8,128)S(1)} %bitcast.71, f32[32]{0:T(128)S(1)} %copy-done.21, f32[8,64,32,64]{1,3,2,0:T(8,128)S(1)} %bitcast.73, f32[8,64,32]{1,2,0:T(8,128)S(1)} %copy-done.13, f32[]{:T(128)} %bitcast.5, f32[8,64,64]{2,1,0:T(8,128)S(1)} %copy-done.11, ...), kind=kOutput, calls=%fused_computation.6 | convolution fusion | flops 148881408 | bytes 12980356 | tf_op jit(solution)/shard_map/ctsh,cshp->cthp/dot_general | solution.py:72
  656.1 7.0 %select_convert_fusion = bf16[8,64,32,64]{1,3,2,0:T(8,128)(2,1)} fusion(f32[8,64,32,64]{1,3,2,0:T(8,128)} %get-tuple-element.60, f32[8,64,32]{1,2,0:T(8,128)S(1)} %add_rsqrt_fusion, pred[8,64]{1,0:T(8,128)(4,1)S(1)} %copy-done.15), kind=kLoop, calls=%fused_computation.5 | loop fusion | flops 3145728 | bytes 6357504 | tf_op jit(solution)/shard_map/convert_element_type | solution.py:137
  663.1 7.1 %copy.51 = bf16[8,64,32,64]{3,2,1,0:T(8,128)(2,1)} copy(bf16[8,64,32,64]{1,3,2,0:T(8,128)(2,1)} %select_convert_fusion) | data formatting | bytes 4194304 | tf_op jit(solution)/shard_map/convert_element_type | solution.py:137
  670.2 6.7 convert_element_type.162
  (102 shorter events, 13.9 us)
Async XLA Ops:
  7.6 15.8 %copy-start.20 = (s32[1,11]{1,0:T(1,128)S(1)}, s32[1,11]{1,0:T(1,128)}, u32[]{:S(2)}) copy-start(s32[1,11]{1,0:T(1,128)} %param.22) | copy-start | bytes 136
  7.6 17.2 %copy-start.14 = (f32[4,2304]{1,0:T(4,128)S(1)}, f32[4,2304]{1,0:T(4,128)}, u32[]{:S(2)}) copy-start(f32[4,2304]{1,0:T(4,128)} %param.19) | copy-start | bytes 110596
  7.6 446.1 %all-to-all-start = ((bf16[256,16,2336]{2,1,0:T(8,128)(2,1)}), bf16[256,16,2336]{2,1,0:T(8,128)(2,1)}, u32[]{:S(2)}, u32[]{:S(2)}) async-start(bf16[256,16,2336]{2,1,0:T(8,128)(2,1)} %stack.2), calls=%async_computation | async-start | bytes 39845888 | tf_op jit(solution)/shard_map/all_to_all | solution.py:14
  453.7 17.8 %copy-start.18 = (f32[32]{0:T(128)S(1)}, f32[32]{0:T(128)}, u32[]{:S(2)}) copy-start(f32[32]{0:T(128)} %param.20) | copy-start | bytes 388
  471.6 12.5 %copy-start.3 = (bf16[512,2336]{0,1:T(8,128)(2,1)}, bf16[512,2336]{0,1:T(8,128)(2,1)S(1)}, u32[]{:S(2)}) copy-start(bf16[512,2336]{0,1:T(8,128)(2,1)S(1)} %get-tuple-element.57) | copy-start | bytes 7176196
  480.7 50.4 %copy-start.16 = (f32[1,32]{1,0:T(1,128)}, f32[1,32]{1,0:T(1,128)S(1)}, u32[]{:S(2)}) copy-start(f32[1,32]{1,0:T(1,128)S(1)} %get-tuple-element.18) | copy-start | bytes 388
  481.2 5.3 copy-start.7
  481.2 6.2 collective-permute-start
  499.7 7.2 %copy-start.8 = (f32[8,64,32]{1,2,0:T(8,128)S(1)}, f32[8,64,32]{1,2,0:T(8,128)}, u32[]{:S(2)}) copy-start(f32[8,64,32]{1,2,0:T(8,128)} %copy.41) | copy-start | bytes 196612
  513.2 3.3 copy-start
  516.4 2.3 copy-start.1
  516.4 0.6 copy-start.17
  518.7 17.6 %collective-permute-start.1 = (bf16[32,128,64]{1,2,0:T(8,128)(2,1)S(1)}, bf16[32,128,64]{1,2,0:T(8,128)(2,1)S(1)}, u32[]{:S(2)}, u32[]{:S(2)}) collective-permute-start(bf16[32,128,64]{1,2,0:T(8,128)(2,1)S(1)} %get-tuple-element.25), channel_id=1, source_target_pairs={{0,8},{8,0},{16,24},{24,16},{32,40},{40,32},{48,56},{56,48},{64,72... | collective-permute-start | bytes 1572872 | tf_op jit(solution)/shard_map/ppermute | solution.py:27
  521.1 10.0 %collective-permute-start.2 = (bf16[32]{0:T(256)(128)(2,1)S(1)}, bf16[32]{0:T(256)(128)(2,1)S(1)}, u32[]{:S(2)}, u32[]{:S(2)}) collective-permute-start(bf16[32]{0:T(256)(128)(2,1)S(1)} %bitcast_convert_fusion), channel_id=1, source_target_pairs={{0,8},{8,0},{16,24},{24,16},{32,40},{40,32},{48,56},{56,48},{64,72... | collective-permute-start | bytes 200 | tf_op jit(solution)/shard_map/ppermute | solution.py:27
  531.1 1.6 copy-start.19
  531.1 4.0 collective-permute-start.4
  536.3 0.8 copy-start.5
  539.4 63.4 %copy-start.6 = (f32[8,64,32]{2,0,1:T(8,128)S(1)}, f32[8,64,32]{2,0,1:T(8,128)}, u32[]{:S(2)}) copy-start(f32[8,64,32]{2,0,1:T(8,128)} %get-tuple-element.27) | copy-start | bytes 196612
  539.4 10.9 %collective-permute-start.3 = (bf16[32,128,64]{1,2,0:T(8,128)(2,1)}, bf16[32,128,64]{1,2,0:T(8,128)(2,1)S(1)}, u32[]{:S(2)}, u32[]{:S(2)}) collective-permute-start(bf16[32,128,64]{1,2,0:T(8,128)(2,1)} %get-tuple-element.15), channel_id=1, source_target_pairs={{0,16},{8,24},{16,0},{24,8},{32,48},{40,56},{48,32},{56,40},{64,80... | collective-permute-start | bytes 1572872 | tf_op jit(solution)/shard_map/ppermute | solution.py:27
  550.7 17.5 %collective-permute-start.5 = (bf16[32,128,64]{1,2,0:T(8,128)(2,1)S(1)}, bf16[32,128,64]{1,2,0:T(8,128)(2,1)S(1)}, u32[]{:S(2)}, u32[]{:S(2)}) collective-permute-start(bf16[32,128,64]{1,2,0:T(8,128)(2,1)S(1)} %fusion.38), channel_id=1, source_target_pairs={{0,32},{8,40},{16,48},{24,56},{32,0},{40,8},{48,16},{56,24},{64,96... | collective-permute-start | bytes 1572872 | tf_op jit(solution)/shard_map/ppermute | solution.py:27
  553.1 6.0 collective-permute-start.6
  559.7 7.2 %collective-permute-start.8 = (bf16[32]{0:T(256)(128)(2,1)S(1)}, bf16[32]{0:T(256)(128)(2,1)S(1)}, u32[]{:S(2)}, u32[]{:S(2)}) collective-permute-start(bf16[32]{0:T(256)(128)(2,1)S(1)} %get-tuple-element.40), channel_id=1, source_target_pairs={{0,64},{8,72},{16,80},{24,88},{32,96},{40,104},{48,112},{56,120},{... | collective-permute-start | bytes 200 | tf_op jit(solution)/shard_map/ppermute | solution.py:27
  570.3 25.3 %collective-permute-start.7 = (bf16[32,128,64]{1,2,0:T(8,128)(2,1)}, bf16[32,128,64]{1,2,0:T(8,128)(2,1)S(1)}, u32[]{:S(2)}, u32[]{:S(2)}) collective-permute-start(bf16[32,128,64]{1,2,0:T(8,128)(2,1)} %fusion.37), channel_id=1, source_target_pairs={{0,64},{8,72},{16,80},{24,88},{32,96},{40,104},{48,112},{56,120},{... | collective-permute-start | bytes 1572872 | tf_op jit(solution)/shard_map/ppermute | solution.py:27
  595.6 2.6 copy-start.4
  598.2 28.4 %collective-permute-start.9 = (bf16[32,128,64]{1,2,0:T(8,128)(2,1)}, bf16[32,128,64]{1,2,0:T(8,128)(2,1)}, u32[]{:S(2)}, u32[]{:S(2)}) collective-permute-start(bf16[32,128,64]{1,2,0:T(8,128)(2,1)} %fusion.28), channel_id=1, source_target_pairs={{0,128},{8,136},{16,144},{24,152},{32,160},{40,168},{48,176},{56,1... | collective-permute-start | bytes 1572872 | tf_op jit(solution)/shard_map/ppermute | solution.py:27
  603.6 0.9 copy-start.10
  603.7 24.9 %copy-start.2 = (f32[32,128,64]{1,2,0:T(8,128)S(1)}, f32[32,128,64]{1,2,0:T(8,128)}, u32[]{:S(2)}) copy-start(f32[32,128,64]{1,2,0:T(8,128)} %get-tuple-element.26) | copy-start | bytes 3145732
  604.7 26.5 %slice-start.3 = ((f32[4,32,128,64]{2,3,1,0:T(8,128)}), f32[3,32,128,64]{2,3,1,0:T(8,128)S(1)}, s32[]{:S(2)}) async-start(f32[4,32,128,64]{2,3,1,0:T(8,128)} %copy-done.1), calls=%async_computation.4 | async-start | bytes 6291456 | tf_op jit(solution)/shard_map/slice | solution.py:87
  631.1 5.4 slice-start
  631.1 16.2 %slice-start.1 = ((s8[8388608]{0:T(1024)(128)(4,1)}), s8[4194304]{0:T(1024)(128)(4,1)S(1)}, s32[]{:S(2)}) async-start(s8[8388608]{0:T(1024)(128)(4,1)} %bitcast.70), calls=%async_computation.2 | async-start | bytes 8388608
  636.5 10.8 %slice-start.2 = ((s8[8388608]{0:T(1024)(128)(4,1)}), s8[4194304]{0:T(1024)(128)(4,1)S(1)}, s32[]{:S(2)}) async-start(s8[8388608]{0:T(1024)(128)(4,1)} %bitcast.70), calls=%async_computation.3 | async-start | bytes 8388608
  643.8 3.6 copy-start.9
  643.8 3.6 copy-start.11
  643.8 3.6 copy-start.12
  643.8 3.6 copy-start.13
  643.8 3.6 copy-start.21
  643.8 3.6 copy-start.22
  647.4 8.7 %copy-start.15 = (pred[8,64]{1,0:T(8,128)(4,1)S(1)}, pred[8,64]{1,0:T(8,128)(4,1)}, u32[]{:S(2)}) copy-start(pred[8,64]{1,0:T(8,128)(4,1)} %add_compare_fusion) | copy-start | bytes 1540
